TPU v7x, 32 devices: a whole 2x2x4 slice. The times are simulated.
32 devices in a mesh: dp: 8 (over y, x, core), seq: 4 (over z).
Axes of the slice: x: 2, y: 2, z: 4, core: 2. Of those that a mesh axis runs over, the one named last changes fastest.
Arguments:
- inputs: bfloat16 [24, 1024, 768], P('dp', 'seq'), may hold values from -6 to 6
- cotangent: bfloat16 [24, 1024, 768], P('dp', 'seq'), may hold values from -6 to 6
- lengths: int32 [24], P('dp'), may hold values from 100 to 1024, as said below
- predicted: int32 [24, 1024], P('dp', 'seq'), may hold values from 0 to 69
- norm1_gain: float32 [768], replicated, may hold values from 0.1 to 1.9
- norm1_shift: float32 [768], replicated, may hold values from -4 to 4
- w_query: bfloat16 [768, 768], replicated, may hold values from -0.3125 to 0.3125
- b_query: float32 [768], replicated, may hold values from -6 to 6
- w_key: bfloat16 [768, 768], replicated, may hold values from -0.3125 to 0.3125
- b_key: float32 [768], replicated, may hold values from -6 to 6
- w_value: bfloat16 [768, 768], replicated, may hold values from -0.21875 to 0.21875
- b_value: float32 [768], replicated, may hold values from -6 to 6
- w_out: bfloat16 [768, 768], replicated, may hold values from -2 to 2
- b_out: float32 [768], replicated, may hold values from -6 to 6
- norm2_gain: float32 [768], replicated, may hold values from 0.1 to 1.9
- norm2_shift: float32 [768], replicated, may hold values from -4 to 4
- w_up: bfloat16 [768, 3072], replicated, may hold values from -0.21875 to 0.21875
- b_up: float32 [3072], replicated, may hold values from -6 to 6
- w_down: bfloat16 [3072, 768], replicated, may hold values from -0.109375 to 0.109375
- b_down: float32 [768], replicated, may hold values from -6 to 6
Outputs:
- result: bfloat16 [24, 1024, 768], P('dp', 'seq')
- grad_inputs: bfloat16 [24, 1024, 768], P('dp', 'seq')
- grad_norm1_gain: float32 [768], replicated
- grad_norm1_shift: float32 [768], replicated
- grad_w_query: float32 [768, 768], replicated
- grad_b_query: float32 [768], replicated
- grad_w_key: float32 [768, 768], replicated
- grad_b_key: float32 [768], replicated
- grad_w_value: float32 [768, 768], replicated
- grad_b_value: float32 [768], replicated
- grad_w_out: float32 [768, 768], replicated
- grad_b_out: float32 [768], replicated
- grad_norm2_gain: float32 [768], replicated
- grad_norm2_shift: float32 [768], replicated
- grad_w_up: float32 [768, 3072], replicated
- grad_b_up: float32 [3072], replicated
- grad_w_down: float32 [3072, 768], replicated
- grad_b_down: float32 [768], replicated
- histogram: int32 [70], replicated
Inputs may be any that keep to these rules, and one draw needn't show every extreme that they name: Some sequence has 1024 real codons and some has 100; the codons from position lengths[s] on are padding.
All inputs are finite; a program needn't handle non-finite values.
Results may differ from a plain program's by a relative error of at most 0.014.
The roundings to bfloat16 on the way count: a program that leaves them out, or rounds other values in their place, can miss the bound.
Values may be sent and summed in bfloat16 or wider, within the bound.
No kernel may reach another device: no remote copies, remote signals or barrier semaphores. Data moves between devices by JAX's collectives and lax.ppermute only.
A program may use at most 192 MiB of HBM per device.

v0:
```python
import jax
import jax.numpy as jnp
from jax import lax
from jax.sharding import PartitionSpec as P

HEAD = 64
CLASSES = 70
epsilon = 1e-05


def matmul(left, right):
    return jnp.dot(left, right, preferred_element_type=jnp.float32)


def matmul_left(left, right):
    return lax.dot_general(
        left, right, (((0,), (0,)), ((), ())), preferred_element_type=jnp.float32
    )


def matmul_right(left, right):
    return lax.dot_general(
        left, right, (((1,), (1,)), ((), ())), preferred_element_type=jnp.float32
    )


def layer_norm(value, gain, shift):
    centre = value - jnp.mean(value, axis=-1, keepdims=True)
    scale = lax.rsqrt(jnp.mean(centre * centre, axis=-1, keepdims=True) + epsilon)
    return centre * scale * gain + shift


def gelu(value):
    return jax.nn.gelu(value, approximate=False)


def rotate(value, direction):
    count = value.shape[-3]
    half = value.shape[-1] // 2
    frequency = 10000.0 ** (-jnp.arange(half, dtype=jnp.float32) / half)
    angle = jnp.arange(count, dtype=jnp.float32)[:, None] * frequency[None, :]
    cosine = jnp.cos(angle)[:, None, :]
    sine = direction * jnp.sin(angle)[:, None, :]
    first = value[..., :half]
    second = value[..., half:]
    return jnp.concatenate(
        [first * cosine - second * sine, second * cosine + first * sine], axis=-1
    )


def attend_forward(query, key, value, valid, block):
    count, heads, size = query.shape
    scale = HEAD ** (-0.5)
    blocks = query.reshape(count // block, block, heads, size)

    def visit(query_block):
        scores = (
            jnp.einsum("qhd,khd->hqk", query_block, key, preferred_element_type=jnp.float32) * scale
        )
        scores = jnp.where(valid[None, None, :], scores, -1e30)
        peak = jnp.max(scores, axis=-1, keepdims=True)
        total = jnp.sum(jnp.exp(scores - peak), axis=-1, keepdims=True)
        logsum = peak + jnp.log(total)
        weights = jnp.exp(scores - logsum).astype(jnp.bfloat16)
        mixed = jnp.einsum("hqk,khd->qhd", weights, value, preferred_element_type=jnp.float32)
        return (mixed.astype(jnp.bfloat16), logsum[..., 0])

    mixed, logsum = lax.map(visit, blocks)
    return (mixed.reshape(count, heads * size), logsum)


def attend_backward(query, key, value, valid, logsum, grad_mixed, block):
    count, heads, size = query.shape
    number = count // block
    scale = HEAD ** (-0.5)
    query_blocks = query.reshape(number, block, heads, size)
    grad_blocks = grad_mixed.reshape(number, block, heads, size)

    def visit(carry, item):
        grad_key, grad_value = carry
        query_block, grad_block, logsum_block = item
        scores = (
            jnp.einsum("qhd,khd->hqk", query_block, key, preferred_element_type=jnp.float32) * scale
        )
        scores = jnp.where(valid[None, None, :], scores, -1e30)
        weights = jnp.exp(scores - logsum_block[..., None])
        weights_low = weights.astype(jnp.bfloat16)
        grad_weights = jnp.einsum(
            "qhd,khd->hqk", grad_block, value, preferred_element_type=jnp.float32
        )
        inner = jnp.sum(weights * grad_weights, axis=-1, keepdims=True)
        grad_scores = (weights * (grad_weights - inner)).astype(jnp.bfloat16)
        grad_query = (
            jnp.einsum("hqk,khd->qhd", grad_scores, key, preferred_element_type=jnp.float32) * scale
        )
        grad_key = (
            grad_key
            + jnp.einsum(
                "hqk,qhd->khd", grad_scores, query_block, preferred_element_type=jnp.float32
            )
            * scale
        )
        grad_value = grad_value + jnp.einsum(
            "hqk,qhd->khd", weights_low, grad_block, preferred_element_type=jnp.float32
        )
        return ((grad_key, grad_value), grad_query)

    start = jnp.zeros((count, heads, size), jnp.float32)
    (grad_key, grad_value), grad_query = lax.scan(
        visit, (start, start), (query_blocks, grad_blocks, logsum)
    )
    grad_query = rotate(grad_query.reshape(count, heads, size), -1.0).astype(jnp.bfloat16)
    grad_key = rotate(grad_key, -1.0).astype(jnp.bfloat16)
    grad_value = grad_value.astype(jnp.bfloat16)
    return (
        grad_query.reshape(count, heads * size),
        grad_key.reshape(count, heads * size),
        grad_value.reshape(count, heads * size),
    )


def on_device(
    inputs,
    cotangent,
    lengths,
    predicted,
    norm1_gain,
    norm1_shift,
    w_query,
    b_query,
    w_key,
    b_key,
    w_value,
    b_value,
    w_out,
    b_out,
    norm2_gain,
    norm2_shift,
    w_up,
    b_up,
    w_down,
    b_down,
):
    seqs, span, width = inputs.shape
    tokens = seqs * span
    hidden_width = w_up.shape[1]
    flat_in = inputs.reshape(tokens, width).astype(jnp.float32)
    normed_full, norm1_back = jax.vjp(layer_norm, flat_in, norm1_gain, norm1_shift)
    normed = normed_full.astype(jnp.bfloat16)
    query = (matmul(normed, w_query) + b_query).astype(jnp.bfloat16).reshape(seqs, span, width)
    key = (matmul(normed, w_key) + b_key).astype(jnp.bfloat16).reshape(seqs, span, width)
    value = (matmul(normed, w_value) + b_value).astype(jnp.bfloat16).reshape(seqs, span, width)
    head_query, head_key, head_value = (
        lax.all_to_all(query, "seq", split_axis=2, concat_axis=1, tiled=True),
        lax.all_to_all(key, "seq", split_axis=2, concat_axis=1, tiled=True),
        lax.all_to_all(value, "seq", split_axis=2, concat_axis=1, tiled=True),
    )
    count = head_query.shape[1]
    heads = head_query.shape[2] // HEAD
    shaped = (seqs, count, heads, HEAD)
    rot_query = rotate(head_query.reshape(shaped).astype(jnp.float32), 1.0).astype(jnp.bfloat16)
    rot_key = rotate(head_key.reshape(shaped).astype(jnp.float32), 1.0).astype(jnp.bfloat16)
    head_value = head_value.reshape(shaped)
    valid = jnp.arange(count)[None, :] < lengths[:, None]
    block = min(count, 512)
    mixed, logsum = lax.map(
        lambda item: attend_forward(item[0], item[1], item[2], item[3], block),
        (rot_query, rot_key, head_value, valid),
    )
    attended = lax.all_to_all(mixed, "seq", split_axis=1, concat_axis=2, tiled=True).reshape(
        tokens, width
    )
    middle = flat_in + matmul(attended, w_out) + b_out
    normed2_full, norm2_back = jax.vjp(layer_norm, middle, norm2_gain, norm2_shift)
    normed2 = normed2_full.astype(jnp.bfloat16)
    hidden_in = matmul(normed2, w_up) + b_up
    hidden = gelu(hidden_in).astype(jnp.bfloat16)
    result = (
        (middle + matmul(hidden, w_down) + b_down).astype(jnp.bfloat16).reshape(seqs, span, width)
    )
    grad_result = cotangent.reshape(tokens, width)
    grad_result_full = grad_result.astype(jnp.float32)
    grad_w_down = matmul_left(hidden, grad_result)
    grad_b_down = jnp.sum(grad_result_full, axis=0)
    unused, gelu_back = jax.vjp(gelu, hidden_in)
    grad_hidden_in = gelu_back(matmul_right(grad_result, w_down))[0].astype(jnp.bfloat16)
    grad_w_up = matmul_left(normed2, grad_hidden_in)
    grad_b_up = jnp.sum(grad_hidden_in.astype(jnp.float32), axis=0)
    grad_from_norm2, grad_norm2_gain, grad_norm2_shift = norm2_back(
        matmul_right(grad_hidden_in, w_up)
    )
    grad_middle = grad_result_full + grad_from_norm2
    grad_branch = grad_middle.astype(jnp.bfloat16)
    grad_w_out = matmul_left(attended, grad_branch)
    grad_b_out = jnp.sum(grad_middle, axis=0)
    grad_attended = matmul_right(grad_branch, w_out).astype(jnp.bfloat16).reshape(seqs, span, width)
    grad_mixed = lax.all_to_all(
        grad_attended, "seq", split_axis=2, concat_axis=1, tiled=True
    ).reshape(shaped)
    grad_query, grad_key, grad_value = lax.map(
        lambda item: attend_backward(item[0], item[1], item[2], item[3], item[4], item[5], block),
        (rot_query, rot_key, head_value, valid, logsum, grad_mixed),
    )
    back_query, back_key, back_value = (
        lax.all_to_all(grad_query, "seq", split_axis=1, concat_axis=2, tiled=True),
        lax.all_to_all(grad_key, "seq", split_axis=1, concat_axis=2, tiled=True),
        lax.all_to_all(grad_value, "seq", split_axis=1, concat_axis=2, tiled=True),
    )
    back_query = back_query.reshape(tokens, width)
    back_key = back_key.reshape(tokens, width)
    back_value = back_value.reshape(tokens, width)
    grad_w_query = matmul_left(normed, back_query)
    grad_w_key = matmul_left(normed, back_key)
    grad_w_value = matmul_left(normed, back_value)
    grad_b_query = jnp.sum(back_query.astype(jnp.float32), axis=0)
    grad_b_key = jnp.sum(back_key.astype(jnp.float32), axis=0)
    grad_b_value = jnp.sum(back_value.astype(jnp.float32), axis=0)
    grad_normed = (
        matmul_right(back_query, w_query)
        + matmul_right(back_key, w_key)
        + matmul_right(back_value, w_value)
    )
    grad_from_norm1, grad_norm1_gain, grad_norm1_shift = norm1_back(grad_normed)
    grad_inputs = (grad_middle + grad_from_norm1).astype(jnp.bfloat16).reshape(seqs, span, width)
    position = lax.axis_index("seq") * span + jnp.arange(span)
    live = position[None, :] < lengths[:, None]
    classes = jnp.arange(CLASSES)
    counts = jnp.sum(
        jnp.where(live[:, :, None] & (predicted[:, :, None] == classes), 1.0, 0.0), axis=(0, 1)
    )
    (
        grad_norm1_gain,
        grad_norm1_shift,
        grad_b_query,
        grad_b_key,
        grad_b_value,
        grad_b_out,
        grad_norm2_gain,
        grad_norm2_shift,
        grad_b_up,
        grad_b_down,
        counts,
    ) = lax.psum(
        (
            grad_norm1_gain,
            grad_norm1_shift,
            grad_b_query,
            grad_b_key,
            grad_b_value,
            grad_b_out,
            grad_norm2_gain,
            grad_norm2_shift,
            grad_b_up,
            grad_b_down,
            counts,
        ),
        ("dp", "seq"),
    )
    part_query = grad_w_query.reshape(-1)
    part_key = grad_w_key.reshape(-1)
    part_value = grad_w_value.reshape(-1)
    part_out = grad_w_out.reshape(-1)
    part_up = grad_w_up.reshape(-1)
    part_down = grad_w_down.reshape(-1)
    part_query, part_key, part_value, part_out, part_up, part_down = (
        lax.psum_scatter(part_query, ("dp", "seq"), scatter_dimension=0, tiled=True),
        lax.psum_scatter(part_key, ("dp", "seq"), scatter_dimension=0, tiled=True),
        lax.psum_scatter(part_value, ("dp", "seq"), scatter_dimension=0, tiled=True),
        lax.psum_scatter(part_out, ("dp", "seq"), scatter_dimension=0, tiled=True),
        lax.psum_scatter(part_up, ("dp", "seq"), scatter_dimension=0, tiled=True),
        lax.psum_scatter(part_down, ("dp", "seq"), scatter_dimension=0, tiled=True),
    )
    part_query, part_key, part_value, part_out, part_up, part_down = (
        lax.all_gather(part_query, ("dp", "seq"), axis=0, tiled=True),
        lax.all_gather(part_key, ("dp", "seq"), axis=0, tiled=True),
        lax.all_gather(part_value, ("dp", "seq"), axis=0, tiled=True),
        lax.all_gather(part_out, ("dp", "seq"), axis=0, tiled=True),
        lax.all_gather(part_up, ("dp", "seq"), axis=0, tiled=True),
        lax.all_gather(part_down, ("dp", "seq"), axis=0, tiled=True),
    )
    return (
        result,
        grad_inputs,
        grad_norm1_gain,
        grad_norm1_shift,
        part_query.reshape(width, width),
        grad_b_query,
        part_key.reshape(width, width),
        grad_b_key,
        part_value.reshape(width, width),
        grad_b_value,
        part_out.reshape(width, width),
        grad_b_out,
        grad_norm2_gain,
        grad_norm2_shift,
        part_up.reshape(width, hidden_width),
        grad_b_up,
        part_down.reshape(hidden_width, width),
        grad_b_down,
        counts.astype(jnp.int32),
    )


def solution(mesh):
    return jax.shard_map(
        on_device,
        mesh=mesh,
        in_specs=(
            P("dp", "seq", None),
            P("dp", "seq", None),
            P("dp"),
            P("dp", "seq"),
            P(),
            P(),
            P(),
            P(),
            P(),
            P(),
            P(),
            P(),
            P(),
            P(),
            P(),
            P(),
            P(),
            P(),
            P(),
            P(),
        ),
        out_specs=(
            P("dp", "seq", None),
            P("dp", "seq", None),
            P(),
            P(),
            P(),
            P(),
            P(),
            P(),
            P(),
            P(),
            P(),
            P(),
            P(),
            P(),
            P(),
            P(),
            P(),
            P(),
            P(),
        ),
        check_vma=False,
    )
```

profile of v0, /device:TPU:0, one launch (start us, length us, event | category | flops | bytes accessed | tf_op | source)
XLA Modules:
  0.0 1592.5 jit_solution(14903146880478550544)
XLA Ops:
  29.5 29.6 %all-to-all-done.1 = bf16[3,256,768]{1,0,2:T(4,128)(2,1)S(1)} async-done(((bf16[3,256,768]{1,0,2:T(4,128)(2,1)}), bf16[3,256,768]{1,0,2:T(4,128)(2,1)S(1)}, u32[]{:S(2)}, u32[]{:S(2)}) %all-to-all-start.1) | async-done | bytes 1179680 | tf_op jit(solution)/shard_map/all_to_all | solution.py:155
  70.5 29.5 %all-to-all-done = bf16[3,256,768]{1,0,2:T(4,128)(2,1)} async-done(((bf16[3,256,768]{1,0,2:T(4,128)(2,1)}), bf16[3,256,768]{1,0,2:T(4,128)(2,1)}, u32[]{:S(2)}, u32[]{:S(2)}) %all-to-all-start) | async-done | bytes 1179680 | tf_op jit(solution)/shard_map/all_to_all | solution.py:154
  116.0 25.4 %all-to-all-done.2 = bf16[3,256,768]{1,0,2:T(4,128)(2,1)} async-done(((bf16[3,256,768]{1,0,2:T(4,128)(2,1)}), bf16[3,256,768]{1,0,2:T(4,128)(2,1)}, u32[]{:S(2)}, u32[]{:S(2)}) %all-to-all-start.2) | async-done | bytes 1179680 | tf_op jit(solution)/shard_map/all_to_all | solution.py:156
  153.6 43.8 %while.54 = (s32[]{:T(128)}, bf16[3,1024,192]{1,2,0:T(8,128)(2,1)}, f32[3,2,3,512]{3,2,1,0:T(4,128)}, bf16[3,1024,3,64]{1,3,2,0:T(8,128)(2,1)}, bf16[3,1024,3,64...) while((s32[]{:T(128)}, bf16[3,1024,192]{1,2,0:T(8,128)(2,1)}, ...), condition=%wide.region_7.8_spmd, body=%wide.region_2.7_spmd.sunk | while | flops 420051456 | bytes 28114308 | solution.py:166
  201.6 51.3 %all_to_all.108 = bf16[3,1024,192]{2,0,1:T(4,128)(2,1)S(1)} all-to-all(bf16[3,1024,192]{2,0,1:T(4,128)(2,1)} %copy.117), channel_id=1, replica_groups=mesh['dp'=8,'seq'=4] {'seq'}, dimensions={1} | all-to-all | bytes 2359296 | tf_op jit(solution)/shard_map/all_to_all | solution.py:170
  269.6 27.3 %convert_reduce_fusion = (f32[3072]{0:T(1024)}, bf16[768,3072]{1,0:T(8,128)(2,1)S(1)}, f32[768,3072]{1,0:T(8,128)}) fusion(f32[768,3072]{1,0:T(8,128)S(1)} %fusion.73, f32[3072]{0:T(1024)S(1)} %copy-done.58, bf16[768,768]{1,0:T(8,128)(2,1)S(1)} %bitcast.247, bf16[3072,768]{1,0:T(8,128)(2,1)S(1)} %bitcast.262), kind=kOutput, calls=%fused_computation.74 | convolution fusion | flops 3800822784 | bytes 29515776 | tf_op jit(solution)/shard_map/dot_general | solution.py:22
  311.3 36.0 %all-to-all-done.4 = bf16[3,256,768]{1,0,2:T(4,128)(2,1)S(1)} async-done(((bf16[3,256,768]{1,0,2:T(4,128)(2,1)}), bf16[3,256,768]{1,0,2:T(4,128)(2,1)S(1)}, u32[]{:S(2)}, u32[]{:S(2)}) %all-to-all-start.4) | async-done | bytes 1179680 | tf_op jit(solution)/shard_map/all_to_all | solution.py:197
  352.8 180.7 %while.56 = (s32[]{:T(128)}, bf16[3,1024,192]{1,2,0:T(8,128)(2,1)}, bf16[3,1024,192]{1,2,0:T(8,128)(2,1)}, bf16[3,1024,192]{1,2,0:T(8,128)(2,1)}, bf16[3,1024,3,...) while((s32[]{:T(128)}, bf16[3,1024,192]{1,2,0:T(8,128)(2,1)}, ...), condition=%wide.region_16.17_spmd, body=%wide.region_12.16_spmd.sunk | while | flops 1034713664 | bytes 145711024 | solution.py:200
  359.7 48.1 %while.58 = (s32[]{:T(128)}, f32[1024,3,64]{0,2,1:T(8,128)S(1)}, f32[1024,3,64]{0,2,1:T(8,128)}, f32[2,512,3,64]{1,0,3,2:T(2,128)}, bf16[2,512,3,64]{1,3,2,0:T(8...) while((s32[]{:T(128)}, f32[1024,3,64]{0,2,1:T(8,128)S(1)}, ...), condition=%wide.region_15.15_spmd.clone, body=%wide.region_13.14_spmd.clone.sunk | while | flops 1031305728 | bytes 117228824 | solution.py:109
  420.0 48.1 %while.58 = (s32[]{:T(128)}, f32[1024,3,64]{0,2,1:T(8,128)S(1)}, f32[1024,3,64]{0,2,1:T(8,128)}, f32[2,512,3,64]{1,0,3,2:T(2,128)}, bf16[2,512,3,64]{1,3,2,0:T(8...) while((s32[]{:T(128)}, f32[1024,3,64]{0,2,1:T(8,128)S(1)}, ...), condition=%wide.region_15.15_spmd.clone, body=%wide.region_13.14_spmd.clone.sunk | while | flops 1031305728 | bytes 117228824 | solution.py:109
  480.2 48.1 %while.58 = (s32[]{:T(128)}, f32[1024,3,64]{0,2,1:T(8,128)S(1)}, f32[1024,3,64]{0,2,1:T(8,128)}, f32[2,512,3,64]{1,0,3,2:T(2,128)}, bf16[2,512,3,64]{1,3,2,0:T(8...) while((s32[]{:T(128)}, f32[1024,3,64]{0,2,1:T(8,128)S(1)}, ...), condition=%wide.region_15.15_spmd.clone, body=%wide.region_13.14_spmd.clone.sunk | while | flops 1031305728 | bytes 117228824 | solution.py:109
  546.2 43.7 %all-to-all-done.7 = bf16[3,1024,192]{2,0,1:T(4,128)(2,1)} async-done(((bf16[3,1024,192]{2,0,1:T(4,128)(2,1)}), bf16[3,1024,192]{2,0,1:T(4,128)(2,1)}, u32[]{:S(2)}, u32[]{:S(2)}) %all-to-all-start.7) | async-done | bytes 1179680 | tf_op jit(solution)/shard_map/all_to_all | solution.py:207
  594.6 10.9 convolution_bitcast_fusion
  605.5 11.0 multiply_convert_fusion.1
  619.0 23.2 %all-to-all-done.5 = bf16[3,1024,192]{2,0,1:T(4,128)(2,1)} async-done(((bf16[3,1024,192]{2,0,1:T(4,128)(2,1)}), bf16[3,1024,192]{2,0,1:T(4,128)(2,1)}, u32[]{:S(2)}, u32[]{:S(2)}) %all-to-all-start.5) | async-done | bytes 1179680 | tf_op jit(solution)/shard_map/all_to_all | solution.py:205
  732.2 436.6 %all-reduce.10.cloned.1.call-done = (f32[589824]{0:T(1024)}, f32[589824]{0:T(1024)}, f32[589824]{0:T(1024)}, f32[589824]{0:T(1024)}, f32[2359296]{0:T(1024)}, /*index=5*/f32[2359296]{0:T(1024)}) async-done(((f32[589824]{0:T(1024)}, f32[589824]{0:T(1024)}, f32[589824]{0:T(1024)}, f32[589824]{0:T(1024)}, f32[2359296]{0:T(1024)}, /*index=5*/f32[2359296]{0:T(1024)}), (f32[589824]{0:T(1024)}, f32[589824]{0:T(1024)}, ...) | async-done | bytes 28311568
  1199.9 41.9 %all-reduce.6 = (f32[768]{0:T(1024)}, f32[768]{0:T(1024)}, f32[768]{0:T(1024)}, f32[768]{0:T(1024)}, f32[768]{0:T(1024)}, /*index=5*/f32[768]{0:T(1024)}, f32[76...) all-reduce(f32[768]{0:T(1024)S(1)} %get-tuple-element.328, ...), channel_id=1, replica_groups=mesh['dp'=8,'seq'=4] {'dp','seq'}, use_global_device_ids=true, to_apply=%region_20.21 | all-reduce | flops 10054 | bytes 80432 | tf_op jit(solution)/shard_map/psum | solution.py:243
  1249.9 38.9 %all-gather.9.cloned.1.call-done = f32[589824]{0:T(1024)} async-done(((f32[18432]{0:T(1024)}), f32[589824]{0:T(1024)}) %all-gather.9.cloned.1.call-update) | async-done | bytes 2359312 | tf_op jit(solution)/shard_map/all_gather | solution.py:275
  1292.1 55.6 %all-gather.11.cloned.1.call-done = f32[589824]{0:T(1024)} async-done(((f32[18432]{0:T(1024)}), f32[589824]{0:T(1024)}) %all-gather.11.cloned.1.call-update) | async-done | bytes 2359312 | tf_op jit(solution)/shard_map/all_gather | solution.py:276
  1351.1 55.6 %all-gather.13.cloned.1.call-done = f32[589824]{0:T(1024)} async-done(((f32[18432]{0:T(1024)}), f32[589824]{0:T(1024)}) %all-gather.13.cloned.1.call-update) | async-done | bytes 2359312 | tf_op jit(solution)/shard_map/all_gather | solution.py:277
  1410.0 80.8 %all-gather.15.cloned.1.call-done = f32[2359296]{0:T(1024)} async-done(((f32[73728]{0:T(1024)}), f32[2359296]{0:T(1024)}) %all-gather.15.cloned.1.call-update) | async-done | bytes 9437200 | tf_op jit(solution)/shard_map/all_gather | solution.py:278
  1490.8 10.9 reshape.501
  1501.7 72.6 %all-gather.17.cloned.1.call-done = f32[2359296]{0:T(1024)} async-done(((f32[73728]{0:T(1024)}), f32[2359296]{0:T(1024)}) %all-gather.17.cloned.1.call-update) | async-done | bytes 9437200 | tf_op jit(solution)/shard_map/all_gather | solution.py:279
  1574.3 11.3 reshape.503
  (542 shorter events, 509.5 us)
Async XLA Ops:
  7.2 56.4 %copy-start = (bf16[768,768]{1,0:T(8,128)(2,1)S(1)}, bf16[768,768]{1,0:T(8,128)(2,1)}, u32[]{:S(2)}) copy-start(bf16[768,768]{1,0:T(8,128)(2,1)} %param.38) | copy-start | bytes 3538948
  15.9 43.3 %all-to-all-start.1 = ((bf16[3,256,768]{1,0,2:T(4,128)(2,1)}), bf16[3,256,768]{1,0,2:T(4,128)(2,1)S(1)}, u32[]{:S(2)}, u32[]{:S(2)}) async-start(bf16[3,256,768]{1,0,2:T(4,128)(2,1)} %copy.111), calls=%async_computation.1 | async-start | bytes 3145728 | tf_op jit(solution)/shard_map/all_to_all | solution.py:155
  59.2 40.9 %all-to-all-start = ((bf16[3,256,768]{1,0,2:T(4,128)(2,1)}), bf16[3,256,768]{1,0,2:T(4,128)(2,1)}, u32[]{:S(2)}, u32[]{:S(2)}) async-start(bf16[3,256,768]{1,0,2:T(4,128)(2,1)} %copy.108), calls=%async_computation | async-start | bytes 3145728 | tf_op jit(solution)/shard_map/all_to_all | solution.py:154
  100.1 41.3 %all-to-all-start.2 = ((bf16[3,256,768]{1,0,2:T(4,128)(2,1)}), bf16[3,256,768]{1,0,2:T(4,128)(2,1)}, u32[]{:S(2)}, u32[]{:S(2)}) async-start(bf16[3,256,768]{1,0,2:T(4,128)(2,1)} %copy.114), calls=%async_computation.2 | async-start | bytes 3145728 | tf_op jit(solution)/shard_map/all_to_all | solution.py:156
  197.4 55.5 %copy-start.7 = (bf16[3,1024,3,64]{1,3,2,0:T(8,128)(2,1)}, bf16[3,1024,3,64]{1,3,2,0:T(8,128)(2,1)S(1)}, u32[]{:S(2)}) copy-start(bf16[3,1024,3,64]{1,3,2,0:T(8,128)(2,1)S(1)} %get-tuple-element.910) | copy-start | bytes 3538948
  197.4 55.5 %copy-start.30 = (pred[3,1024]{1,0:T(4,128)(4,1)}, pred[3,1024]{1,0:T(4,128)(4,1)S(1)}, u32[]{:S(2)}) copy-start(pred[3,1024]{1,0:T(4,128)(4,1)S(1)} %get-tuple-element.943) | copy-start | bytes 9220
  261.6 40.2 %copy-start.8 = (f32[768,768]{1,0:T(8,128)}, f32[768,768]{1,0:T(8,128)S(1)}, u32[]{:S(2)}) copy-start(f32[768,768]{1,0:T(8,128)S(1)} %get-tuple-element.462) | copy-start | bytes 7077892
  261.7 40.1 %copy-start.35 = (f32[768]{0:T(1024)}, f32[768]{0:T(1024)S(1)}, u32[]{:S(2)}) copy-start(f32[768]{0:T(1024)S(1)} %broadcast_multiply_fusion) | copy-start | bytes 9220
  307.3 40.0 %all-to-all-start.4 = ((bf16[3,256,768]{1,0,2:T(4,128)(2,1)}), bf16[3,256,768]{1,0,2:T(4,128)(2,1)S(1)}, u32[]{:S(2)}, u32[]{:S(2)}) async-start(bf16[3,256,768]{1,0,2:T(4,128)(2,1)} %copy.119), calls=%async_computation.4 | async-start | bytes 3145728 | tf_op jit(solution)/shard_map/all_to_all | solution.py:197
  537.5 52.3 %all-to-all-start.7 = ((bf16[3,1024,192]{2,0,1:T(4,128)(2,1)}), bf16[3,1024,192]{2,0,1:T(4,128)(2,1)}, u32[]{:S(2)}, u32[]{:S(2)}) async-start(bf16[3,1024,192]{2,0,1:T(4,128)(2,1)} %copy.126), calls=%async_computation.7 | async-start | bytes 4194304 | tf_op jit(solution)/shard_map/all_to_all | solution.py:207
  546.2 48.4 %copy-start.36 = (f32[768]{0:T(1024)S(1)}, f32[768]{0:T(1024)}, u32[]{:S(2)}) copy-start(f32[768]{0:T(1024)} %copy-done.35) | copy-start | bytes 9220
  546.2 48.4 %copy-start.38 = (f32[768]{0:T(1024)S(1)}, f32[768]{0:T(1024)}, u32[]{:S(2)}) copy-start(f32[768]{0:T(1024)} %copy-done.37) | copy-start | bytes 9220
  546.2 48.4 %copy-start.40 = (f32[768]{0:T(1024)S(1)}, f32[768]{0:T(1024)}, u32[]{:S(2)}) copy-start(f32[768]{0:T(1024)} %param.42) | copy-start | bytes 9220
  546.2 48.4 %copy-start.42 = (f32[768]{0:T(1024)S(1)}, f32[768]{0:T(1024)}, u32[]{:S(2)}) copy-start(f32[768]{0:T(1024)} %param.43) | copy-start | bytes 9220
  589.8 52.4 %all-to-all-start.5 = ((bf16[3,1024,192]{2,0,1:T(4,128)(2,1)}), bf16[3,1024,192]{2,0,1:T(4,128)(2,1)}, u32[]{:S(2)}, u32[]{:S(2)}) async-start(bf16[3,1024,192]{2,0,1:T(4,128)(2,1)} %copy.122), calls=%async_computation.5 | async-start | bytes 4194304 | tf_op jit(solution)/shard_map/all_to_all | solution.py:205
  642.2 58.4 %all-to-all-start.6 = ((bf16[3,1024,192]{2,0,1:T(4,128)(2,1)}), bf16[3,1024,192]{2,0,1:T(4,128)(2,1)}, u32[]{:S(2)}, u32[]{:S(2)}) async-start(bf16[3,1024,192]{2,0,1:T(4,128)(2,1)} %copy.124), calls=%async_computation.6 | async-start | bytes 4194304 | tf_op jit(solution)/shard_map/all_to_all | solution.py:206
  646.7 522.1 %all-reduce.10.cloned.1.call-start = ((), (), s32[]{:S(2)}) async-start(), calls=%async_computation.14 | async-start | bytes 56623104
  732.1 447.3 %copy-start.63 = (s32[3,256]{1,0:T(4,128)S(1)}, s32[3,256]{1,0:T(4,128)}, u32[]{:S(2)}) copy-start(s32[3,256]{1,0:T(4,128)} %param.31) | copy-start | bytes 9220
  732.1 514.4 %all-gather.7.cloned.1.call-start = ((), (), s32[]{:S(2)}) async-start(), calls=%async_computation.8 | async-start | bytes 2433024 | tf_op jit(solution)/shard_map/all_gather | solution.py:274
  1170.3 118.5 %all-gather.9.cloned.1.call-start = ((), (), s32[]{:S(2)}) async-start(), calls=%async_computation.9 | async-start | bytes 2433024 | tf_op jit(solution)/shard_map/all_gather | solution.py:275
  1171.9 175.8 %all-gather.11.cloned.1.call-start = ((), (), s32[]{:S(2)}) async-start(), calls=%async_computation.10 | async-start | bytes 2433024 | tf_op jit(solution)/shard_map/all_gather | solution.py:276
  1173.5 233.1 %all-gather.13.cloned.1.call-start = ((), (), s32[]{:S(2)}) async-start(), calls=%async_computation.11 | async-start | bytes 2433024 | tf_op jit(solution)/shard_map/all_gather | solution.py:277
  1175.1 315.7 %all-gather.15.cloned.1.call-start = ((), (), s32[]{:S(2)}) async-start(), calls=%async_computation.12 | async-start | bytes 9732096 | tf_op jit(solution)/shard_map/all_gather | solution.py:278
  1176.9 397.4 %all-gather.17.cloned.1.call-start = ((), (), s32[]{:S(2)}) async-start(), calls=%async_computation.13 | async-start | bytes 9732096 | tf_op jit(solution)/shard_map/all_gather | solution.py:279
  (110 other events, 564.9 us)
Sparse Core Ops, SparseCore 0:
  732.3 436.4 all-reduce.9
  1172.1 57.0 all-gather.6
  1232.6 56.1 all-gather.8
  1291.5 56.2 all-gather.10
  1350.4 56.2 all-gather.12
  1409.8 80.9 all-gather.14
  1493.6 80.6 all-gather.16
where the time goes:
time: 1600 us; the launch traced here: 1590 us
  waiting for transfers between devices  928 us (58%)
  local copies, waits for them, and re-layouts  257 us (16%)
  matrix products  188 us (12%)
  blocking collectives  93.2 us (6%)
  other arithmetic  77.4 us (5%)
  starting transfers between devices  33.4 us (2%)
    unnamed x8, waiting for transfers between devices  437 us
    all_gather x1, waiting for transfers between devices, on_device(): lax.all_gather(part_up, ('dp', 'seq'), axis=0, tiled=True)  80.8 us
    all_gather x1, waiting for transfers between devices, on_device(): lax.all_gather(part_down, ('dp', 'seq'), axis=0, tiled=True)  72.6 us
    all_gather x1, waiting for transfers between devices, on_device(): lax.all_gather(part_value, ('dp', 'seq'), axis=0, tiled=True)  55.6 us
    all_gather x1, waiting for transfers between devices, on_device(): lax.all_gather(part_out, ('dp', 'seq'), axis=0, tiled=True)  55.6 us
    all_to_all x1, blocking collectives, on_device(): lax.all_to_all(mixed, 'seq', split_axis=1, concat_axis=2, tiled=True)  51.3 us
    dynamic_update_slice x12, local copies, waits for them, and re-layouts, attend_backward(): lax.scan(visit, (start, start), (query_blocks, grad_blocks, logsum))  50.6 us
    all_to_all x1, waiting for transfers between devices, on_device(): lax.all_to_all(grad_value, 'seq', split_axis=1, concat_axis=2, tiled=True)  43.7 us
  transfers between devices with their start and end apart: 14, of which 12 were waited for; matrix products, arithmetic and copies ran while one was open for 10% of the time, Pallas kernels for 0%

commit v1 on v0

--- a/solution.py
+++ b/solution.py
@@ -241,20 +241,23 @@
         grad_b_down,
         counts,
     ) = lax.psum(
-        (
-            grad_norm1_gain,
-            grad_norm1_shift,
-            grad_b_query,
-            grad_b_key,
-            grad_b_value,
-            grad_b_out,
-            grad_norm2_gain,
-            grad_norm2_shift,
-            grad_b_up,
-            grad_b_down,
-            counts,
+        lax.psum(
+            (
+                grad_norm1_gain,
+                grad_norm1_shift,
+                grad_b_query,
+                grad_b_key,
+                grad_b_value,
+                grad_b_out,
+                grad_norm2_gain,
+                grad_norm2_shift,
+                grad_b_up,
+                grad_b_down,
+                counts,
+            ),
+            "dp",
         ),
-        ("dp", "seq"),
+        "seq",
     )
     part_query = grad_w_query.reshape(-1)
     part_key = grad_w_key.reshape(-1)

time: 1600 us -> 1600 us (level)
    psum x0 -> x1, blocking collectives: none -> 18.9 us  [on_device(): lax.psum(lax.psum((grad_norm1_gain, grad_norm1_shift, grad_b_query, grad_...]
    psum x1, blocking collectives: 41.9 us -> 24.7 us  [on_device(): lax.psum((grad_norm1_gain, grad_norm1_shift, grad_b_query, grad_b_key, gr...]
where the time goes in v1:
time: 1600 us; the launch traced here: 1590 us
  waiting for transfers between devices  926 us (58%)
  local copies, waits for them, and re-layouts  257 us (16%)
  matrix products  188 us (12%)
  blocking collectives  94.9 us (6%)
  other arithmetic  77.5 us (5%)
  starting transfers between devices  33.4 us (2%)
    unnamed x8, waiting for transfers between devices  437 us
    all_gather x1, waiting for transfers between devices, on_device(): lax.all_gather(part_up, ('dp', 'seq'), axis=0, tiled=True)  80.8 us
    all_gather x1, waiting for transfers between devices, on_device(): lax.all_gather(part_down, ('dp', 'seq'), axis=0, tiled=True)  72.6 us
    all_gather x1, waiting for transfers between devices, on_device(): lax.all_gather(part_value, ('dp', 'seq'), axis=0, tiled=True)  55.6 us
    all_gather x1, waiting for transfers between devices, on_device(): lax.all_gather(part_out, ('dp', 'seq'), axis=0, tiled=True)  55.6 us
    all_to_all x1, blocking collectives, on_device(): lax.all_to_all(mixed, 'seq', split_axis=1, concat_axis=2, tiled=True)  51.3 us
    dynamic_update_slice x12, local copies, waits for them, and re-layouts, attend_backward(): lax.scan(visit, (start, start), (query_blocks, grad_blocks, logsum))  50.6 us
    all_to_all x1, waiting for transfers between devices, on_device(): lax.all_to_all(grad_value, 'seq', split_axis=1, concat_axis=2, tiled=True)  43.7 us
  transfers between devices with their start and end apart: 14, of which 12 were waited for; matrix products, arithmetic and copies ran while one was open for 10% of the time, Pallas kernels for 0%

profile of v1, /device:TPU:0, one launch (start us, length us, event | category | flops | bytes accessed | tf_op | source)
XLA Modules:
  0.0 1592.9 jit_solution(17513533751428105171)
XLA Ops:
  29.5 29.6 %all-to-all-done.1 = bf16[3,256,768]{1,0,2:T(4,128)(2,1)S(1)} async-done(((bf16[3,256,768]{1,0,2:T(4,128)(2,1)}), bf16[3,256,768]{1,0,2:T(4,128)(2,1)S(1)}, u32[]{:S(2)}, u32[]{:S(2)}) %all-to-all-start.1) | async-done | bytes 1179680 | tf_op jit(solution)/shard_map/all_to_all | solution.py:155
  70.5 29.5 %all-to-all-done = bf16[3,256,768]{1,0,2:T(4,128)(2,1)} async-done(((bf16[3,256,768]{1,0,2:T(4,128)(2,1)}), bf16[3,256,768]{1,0,2:T(4,128)(2,1)}, u32[]{:S(2)}, u32[]{:S(2)}) %all-to-all-start) | async-done | bytes 1179680 | tf_op jit(solution)/shard_map/all_to_all | solution.py:154
  116.0 25.4 %all-to-all-done.2 = bf16[3,256,768]{1,0,2:T(4,128)(2,1)} async-done(((bf16[3,256,768]{1,0,2:T(4,128)(2,1)}), bf16[3,256,768]{1,0,2:T(4,128)(2,1)}, u32[]{:S(2)}, u32[]{:S(2)}) %all-to-all-start.2) | async-done | bytes 1179680 | tf_op jit(solution)/shard_map/all_to_all | solution.py:156
  153.5 43.8 %while.54 = (s32[]{:T(128)}, bf16[3,1024,192]{1,2,0:T(8,128)(2,1)}, f32[3,2,3,512]{3,2,1,0:T(4,128)}, bf16[3,1024,3,64]{1,3,2,0:T(8,128)(2,1)}, bf16[3,1024,3,64...) while((s32[]{:T(128)}, bf16[3,1024,192]{1,2,0:T(8,128)(2,1)}, ...), condition=%wide.region_7.8_spmd, body=%wide.region_2.7_spmd.sunk | while | flops 420051456 | bytes 28114308 | solution.py:166
  201.6 51.3 %all_to_all.108 = bf16[3,1024,192]{2,0,1:T(4,128)(2,1)S(1)} all-to-all(bf16[3,1024,192]{2,0,1:T(4,128)(2,1)} %copy.117), channel_id=1, replica_groups=mesh['dp'=8,'seq'=4] {'seq'}, dimensions={1} | all-to-all | bytes 2359296 | tf_op jit(solution)/shard_map/all_to_all | solution.py:170
  269.6 27.3 %convert_reduce_fusion = (f32[3072]{0:T(1024)}, bf16[768,3072]{1,0:T(8,128)(2,1)S(1)}, f32[768,3072]{1,0:T(8,128)}) fusion(f32[768,3072]{1,0:T(8,128)S(1)} %fusion.73, f32[3072]{0:T(1024)S(1)} %copy-done.58, bf16[768,768]{1,0:T(8,128)(2,1)S(1)} %bitcast.247, bf16[3072,768]{1,0:T(8,128)(2,1)S(1)} %bitcast.262), kind=kOutput, calls=%fused_computation.74 | convolution fusion | flops 3800822784 | bytes 29515776 | tf_op jit(solution)/shard_map/dot_general | solution.py:22
  311.3 36.0 %all-to-all-done.4 = bf16[3,256,768]{1,0,2:T(4,128)(2,1)S(1)} async-done(((bf16[3,256,768]{1,0,2:T(4,128)(2,1)}), bf16[3,256,768]{1,0,2:T(4,128)(2,1)S(1)}, u32[]{:S(2)}, u32[]{:S(2)}) %all-to-all-start.4) | async-done | bytes 1179680 | tf_op jit(solution)/shard_map/all_to_all | solution.py:197
  352.7 180.8 %while.56 = (s32[]{:T(128)}, bf16[3,1024,192]{1,2,0:T(8,128)(2,1)}, bf16[3,1024,192]{1,2,0:T(8,128)(2,1)}, bf16[3,1024,192]{1,2,0:T(8,128)(2,1)}, bf16[3,1024,3,...) while((s32[]{:T(128)}, bf16[3,1024,192]{1,2,0:T(8,128)(2,1)}, ...), condition=%wide.region_16.17_spmd, body=%wide.region_12.16_spmd.sunk | while | flops 1034713664 | bytes 145711024 | solution.py:200
  359.8 48.1 %while.58 = (s32[]{:T(128)}, f32[1024,3,64]{0,2,1:T(8,128)S(1)}, f32[1024,3,64]{0,2,1:T(8,128)}, f32[2,512,3,64]{1,0,3,2:T(2,128)}, bf16[2,512,3,64]{1,3,2,0:T(8...) while((s32[]{:T(128)}, f32[1024,3,64]{0,2,1:T(8,128)S(1)}, ...), condition=%wide.region_15.15_spmd.clone, body=%wide.region_13.14_spmd.clone.sunk | while | flops 1031305728 | bytes 117228824 | solution.py:109
  420.0 48.1 %while.58 = (s32[]{:T(128)}, f32[1024,3,64]{0,2,1:T(8,128)S(1)}, f32[1024,3,64]{0,2,1:T(8,128)}, f32[2,512,3,64]{1,0,3,2:T(2,128)}, bf16[2,512,3,64]{1,3,2,0:T(8...) while((s32[]{:T(128)}, f32[1024,3,64]{0,2,1:T(8,128)S(1)}, ...), condition=%wide.region_15.15_spmd.clone, body=%wide.region_13.14_spmd.clone.sunk | while | flops 1031305728 | bytes 117228824 | solution.py:109
  480.3 48.1 %while.58 = (s32[]{:T(128)}, f32[1024,3,64]{0,2,1:T(8,128)S(1)}, f32[1024,3,64]{0,2,1:T(8,128)}, f32[2,512,3,64]{1,0,3,2:T(2,128)}, bf16[2,512,3,64]{1,3,2,0:T(8...) while((s32[]{:T(128)}, f32[1024,3,64]{0,2,1:T(8,128)S(1)}, ...), condition=%wide.region_15.15_spmd.clone, body=%wide.region_13.14_spmd.clone.sunk | while | flops 1031305728 | bytes 117228824 | solution.py:109
  546.3 43.7 %all-to-all-done.7 = bf16[3,1024,192]{2,0,1:T(4,128)(2,1)} async-done(((bf16[3,1024,192]{2,0,1:T(4,128)(2,1)}), bf16[3,1024,192]{2,0,1:T(4,128)(2,1)}, u32[]{:S(2)}, u32[]{:S(2)}) %all-to-all-start.7) | async-done | bytes 1179680 | tf_op jit(solution)/shard_map/all_to_all | solution.py:207
  605.6 11.0 multiply_convert_fusion.1
  619.1 23.2 %all-to-all-done.5 = bf16[3,1024,192]{2,0,1:T(4,128)(2,1)} async-done(((bf16[3,1024,192]{2,0,1:T(4,128)(2,1)}), bf16[3,1024,192]{2,0,1:T(4,128)(2,1)}, u32[]{:S(2)}, u32[]{:S(2)}) %all-to-all-start.5) | async-done | bytes 1179680 | tf_op jit(solution)/shard_map/all_to_all | solution.py:205
  732.3 436.6 %all-reduce.11.cloned.1.call-done = (f32[589824]{0:T(1024)}, f32[589824]{0:T(1024)}, f32[589824]{0:T(1024)}, f32[589824]{0:T(1024)}, f32[2359296]{0:T(1024)}, /*index=5*/f32[2359296]{0:T(1024)}) async-done(((f32[589824]{0:T(1024)}, f32[589824]{0:T(1024)}, f32[589824]{0:T(1024)}, f32[589824]{0:T(1024)}, f32[2359296]{0:T(1024)}, /*index=5*/f32[2359296]{0:T(1024)}), (f32[589824]{0:T(1024)}, f32[589824]{0:T(1024)}, ...) | async-done | bytes 28311568
  1200.0 24.7 %all-reduce.7 = (f32[768]{0:T(1024)S(1)}, f32[768]{0:T(1024)S(1)}, f32[768]{0:T(1024)S(1)}, f32[768]{0:T(1024)S(1)}, f32[768]{0:T(1024)S(1)}, /*index=5*/f32[768...) all-reduce(f32[768]{0:T(1024)S(1)} %get-tuple-element.328, ...), channel_id=1, replica_groups=mesh['dp'=8,'seq'=4] {'dp'}, use_global_device_ids=true, to_apply=%region_20.21 | all-reduce | flops 10054 | bytes 80432 | tf_op jit(solution)/shard_map/psum | solution.py:244
  1224.8 18.9 %all-reduce.8 = (f32[768]{0:T(1024)}, f32[768]{0:T(1024)}, f32[768]{0:T(1024)}, f32[768]{0:T(1024)}, f32[768]{0:T(1024)}, /*index=5*/f32[768]{0:T(1024)}, f32[76...) all-reduce(f32[768]{0:T(1024)S(1)} %get-tuple-element.407, ...), channel_id=1, replica_groups=mesh['dp'=8,'seq'=4] {'seq'}, use_global_device_ids=true, to_apply=%region_21.22 | all-reduce | flops 10054 | bytes 80432 | tf_op jit(solution)/shard_map/psum | solution.py:243
  1251.8 37.4 %all-gather.9.cloned.1.call-done = f32[589824]{0:T(1024)} async-done(((f32[18432]{0:T(1024)}), f32[589824]{0:T(1024)}) %all-gather.9.cloned.1.call-update) | async-done | bytes 2359312 | tf_op jit(solution)/shard_map/all_gather | solution.py:278
  1292.5 55.6 %all-gather.11.cloned.1.call-done = f32[589824]{0:T(1024)} async-done(((f32[18432]{0:T(1024)}), f32[589824]{0:T(1024)}) %all-gather.11.cloned.1.call-update) | async-done | bytes 2359312 | tf_op jit(solution)/shard_map/all_gather | solution.py:279
  1351.4 55.6 %all-gather.13.cloned.1.call-done = f32[589824]{0:T(1024)} async-done(((f32[18432]{0:T(1024)}), f32[589824]{0:T(1024)}) %all-gather.13.cloned.1.call-update) | async-done | bytes 2359312 | tf_op jit(solution)/shard_map/all_gather | solution.py:280
  1410.3 80.8 %all-gather.15.cloned.1.call-done = f32[2359296]{0:T(1024)} async-done(((f32[73728]{0:T(1024)}), f32[2359296]{0:T(1024)}) %all-gather.15.cloned.1.call-update) | async-done | bytes 9437200 | tf_op jit(solution)/shard_map/all_gather | solution.py:281
  1491.2 10.9 reshape.501
  1502.1 72.6 %all-gather.17.cloned.1.call-done = f32[2359296]{0:T(1024)} async-done(((f32[73728]{0:T(1024)}), f32[2359296]{0:T(1024)}) %all-gather.17.cloned.1.call-update) | async-done | bytes 9437200 | tf_op jit(solution)/shard_map/all_gather | solution.py:282
  1574.6 11.3 reshape.503
  (543 shorter events, 520.6 us)
Async XLA Ops:
  7.2 56.4 %copy-start = (bf16[768,768]{1,0:T(8,128)(2,1)S(1)}, bf16[768,768]{1,0:T(8,128)(2,1)}, u32[]{:S(2)}) copy-start(bf16[768,768]{1,0:T(8,128)(2,1)} %param.38) | copy-start | bytes 3538948
  15.9 43.3 %all-to-all-start.1 = ((bf16[3,256,768]{1,0,2:T(4,128)(2,1)}), bf16[3,256,768]{1,0,2:T(4,128)(2,1)S(1)}, u32[]{:S(2)}, u32[]{:S(2)}) async-start(bf16[3,256,768]{1,0,2:T(4,128)(2,1)} %copy.111), calls=%async_computation.1 | async-start | bytes 3145728 | tf_op jit(solution)/shard_map/all_to_all | solution.py:155
  59.2 40.9 %all-to-all-start = ((bf16[3,256,768]{1,0,2:T(4,128)(2,1)}), bf16[3,256,768]{1,0,2:T(4,128)(2,1)}, u32[]{:S(2)}, u32[]{:S(2)}) async-start(bf16[3,256,768]{1,0,2:T(4,128)(2,1)} %copy.108), calls=%async_computation | async-start | bytes 3145728 | tf_op jit(solution)/shard_map/all_to_all | solution.py:154
  100.1 41.3 %all-to-all-start.2 = ((bf16[3,256,768]{1,0,2:T(4,128)(2,1)}), bf16[3,256,768]{1,0,2:T(4,128)(2,1)}, u32[]{:S(2)}, u32[]{:S(2)}) async-start(bf16[3,256,768]{1,0,2:T(4,128)(2,1)} %copy.114), calls=%async_computation.2 | async-start | bytes 3145728 | tf_op jit(solution)/shard_map/all_to_all | solution.py:156
  197.4 55.5 %copy-start.7 = (bf16[3,1024,3,64]{1,3,2,0:T(8,128)(2,1)}, bf16[3,1024,3,64]{1,3,2,0:T(8,128)(2,1)S(1)}, u32[]{:S(2)}) copy-start(bf16[3,1024,3,64]{1,3,2,0:T(8,128)(2,1)S(1)} %get-tuple-element.921) | copy-start | bytes 3538948
  197.4 55.5 %copy-start.30 = (pred[3,1024]{1,0:T(4,128)(4,1)}, pred[3,1024]{1,0:T(4,128)(4,1)S(1)}, u32[]{:S(2)}) copy-start(pred[3,1024]{1,0:T(4,128)(4,1)S(1)} %get-tuple-element.954) | copy-start | bytes 9220
  261.6 40.2 %copy-start.8 = (f32[768,768]{1,0:T(8,128)}, f32[768,768]{1,0:T(8,128)S(1)}, u32[]{:S(2)}) copy-start(f32[768,768]{1,0:T(8,128)S(1)} %get-tuple-element.473) | copy-start | bytes 7077892
  261.7 40.1 %copy-start.35 = (f32[768]{0:T(1024)}, f32[768]{0:T(1024)S(1)}, u32[]{:S(2)}) copy-start(f32[768]{0:T(1024)S(1)} %broadcast_multiply_fusion) | copy-start | bytes 9220
  307.3 40.0 %all-to-all-start.4 = ((bf16[3,256,768]{1,0,2:T(4,128)(2,1)}), bf16[3,256,768]{1,0,2:T(4,128)(2,1)S(1)}, u32[]{:S(2)}, u32[]{:S(2)}) async-start(bf16[3,256,768]{1,0,2:T(4,128)(2,1)} %copy.119), calls=%async_computation.4 | async-start | bytes 3145728 | tf_op jit(solution)/shard_map/all_to_all | solution.py:197
  537.6 52.4 %all-to-all-start.7 = ((bf16[3,1024,192]{2,0,1:T(4,128)(2,1)}), bf16[3,1024,192]{2,0,1:T(4,128)(2,1)}, u32[]{:S(2)}, u32[]{:S(2)}) async-start(bf16[3,1024,192]{2,0,1:T(4,128)(2,1)} %copy.126), calls=%async_computation.7 | async-start | bytes 4194304 | tf_op jit(solution)/shard_map/all_to_all | solution.py:207
  546.3 48.4 %copy-start.36 = (f32[768]{0:T(1024)S(1)}, f32[768]{0:T(1024)}, u32[]{:S(2)}) copy-start(f32[768]{0:T(1024)} %copy-done.35) | copy-start | bytes 9220
  546.3 48.4 %copy-start.38 = (f32[768]{0:T(1024)S(1)}, f32[768]{0:T(1024)}, u32[]{:S(2)}) copy-start(f32[768]{0:T(1024)} %copy-done.37) | copy-start | bytes 9220
  546.3 48.4 %copy-start.40 = (f32[768]{0:T(1024)S(1)}, f32[768]{0:T(1024)}, u32[]{:S(2)}) copy-start(f32[768]{0:T(1024)} %param.42) | copy-start | bytes 9220
  546.3 48.4 %copy-start.42 = (f32[768]{0:T(1024)S(1)}, f32[768]{0:T(1024)}, u32[]{:S(2)}) copy-start(f32[768]{0:T(1024)} %param.43) | copy-start | bytes 9220
  590.0 52.4 %all-to-all-start.5 = ((bf16[3,1024,192]{2,0,1:T(4,128)(2,1)}), bf16[3,1024,192]{2,0,1:T(4,128)(2,1)}, u32[]{:S(2)}, u32[]{:S(2)}) async-start(bf16[3,1024,192]{2,0,1:T(4,128)(2,1)} %copy.122), calls=%async_computation.5 | async-start | bytes 4194304 | tf_op jit(solution)/shard_map/all_to_all | solution.py:205
  642.4 58.4 %all-to-all-start.6 = ((bf16[3,1024,192]{2,0,1:T(4,128)(2,1)}), bf16[3,1024,192]{2,0,1:T(4,128)(2,1)}, u32[]{:S(2)}, u32[]{:S(2)}) async-start(bf16[3,1024,192]{2,0,1:T(4,128)(2,1)} %copy.124), calls=%async_computation.6 | async-start | bytes 4194304 | tf_op jit(solution)/shard_map/all_to_all | solution.py:206
  646.8 522.1 %all-reduce.11.cloned.1.call-start = ((), (), s32[]{:S(2)}) async-start(), calls=%async_computation.14 | async-start | bytes 56623104
  732.3 447.3 %copy-start.63 = (s32[3,256]{1,0:T(4,128)S(1)}, s32[3,256]{1,0:T(4,128)}, u32[]{:S(2)}) copy-start(s32[3,256]{1,0:T(4,128)} %param.31) | copy-start | bytes 9220
  732.3 516.1 %all-gather.7.cloned.1.call-start = ((), (), s32[]{:S(2)}) async-start(), calls=%async_computation.8 | async-start | bytes 2433024 | tf_op jit(solution)/shard_map/all_gather | solution.py:277
  1170.4 118.7 %all-gather.9.cloned.1.call-start = ((), (), s32[]{:S(2)}) async-start(), calls=%async_computation.9 | async-start | bytes 2433024 | tf_op jit(solution)/shard_map/all_gather | solution.py:278
  1172.0 176.0 %all-gather.11.cloned.1.call-start = ((), (), s32[]{:S(2)}) async-start(), calls=%async_computation.10 | async-start | bytes 2433024 | tf_op jit(solution)/shard_map/all_gather | solution.py:279
  1173.6 233.3 %all-gather.13.cloned.1.call-start = ((), (), s32[]{:S(2)}) async-start(), calls=%async_computation.11 | async-start | bytes 2433024 | tf_op jit(solution)/shard_map/all_gather | solution.py:280
  1175.2 315.9 %all-gather.15.cloned.1.call-start = ((), (), s32[]{:S(2)}) async-start(), calls=%async_computation.12 | async-start | bytes 9732096 | tf_op jit(solution)/shard_map/all_gather | solution.py:281
  1177.0 397.6 %all-gather.17.cloned.1.call-start = ((), (), s32[]{:S(2)}) async-start(), calls=%async_computation.13 | async-start | bytes 9732096 | tf_op jit(solution)/shard_map/all_gather | solution.py:282
  (110 other events, 565.0 us)
Sparse Core Ops, SparseCore 0:
  732.4 436.4 all-reduce.10
  1172.3 57.2 all-gather.6
  1233.0 56.1 all-gather.8
  1291.8 56.2 all-gather.10
  1350.7 56.2 all-gather.12
  1410.2 80.9 all-gather.14
  1494.0 80.6 all-gather.16
